TPU v7x, 256 devices: a whole 4x4x8 slice. The times are simulated.
256 devices in a mesh: gx: 8 (over z_lo, x), gy: 32 (over z_hi, y, core).
Axes of the slice: x: 4, y: 4, z: 8 (z_hi: 4, z_lo: 2; z = z_hi * 2 + z_lo), core: 2. Of those that a mesh axis runs over, the one named last changes fastest.
Arguments:
- velocity: float32 [3, 32, 128, 4096], P(None, None, 'gx', 'gy'), may hold values from -6 to 6
- viscosity: float32 [32, 128, 4096], P(None, 'gx', 'gy'), may hold values from 0.02 to 0.12
- marker_cells: int32 [8192, 3, 128], P(('gx', 'gy')), may hold values from 0 to 4095, as said below
- marker_offset: float32 [8192, 3, 128], P(('gx', 'gy')), may hold values from 0 to 1
- marker_force: float32 [8192, 3, 128], P(('gx', 'gy')), may hold values from -24 to 24
Outputs:
- fluid_velocity: float32 [3, 32, 128, 4096], P(None, None, 'gx', 'gy')
- marker_velocity: float32 [8192, 3, 128], P(('gx', 'gy'))
Inputs may be any that keep to these rules, and one draw needn't show every extreme that they name: `marker_cells`: within one block every marker's x lies in [i * 16, (i + 1) * 16) where i is the gx index of the device holding the block, every marker's y lies in one range [j * 128, (j + 1) * 128), and z lies in [1, 29]. One device holds at most 2 blocks whose y range is one given j, and in every gx column some j receives exactly 2 blocks from every device of that column.
All inputs are finite; a program needn't handle non-finite values.
Results may differ from a plain program's by a relative error of at most 0.0003.
The roundings to bfloat16 on the way count: a program that leaves them out, or rounds other values in their place, can miss the bound.
Values may be sent and summed in bfloat16 or wider, within the bound.
A program may use at most 128 MiB of HBM per device.

v0:
```python
import jax
import jax.numpy as jnp
from jax import lax
from jax.sharding import PartitionSpec as P

CAP = 2
OFFSETS = (-1, 0, 1, 2)
group_slots = 4


def padded_2(array, sides, width):
    for axis, dim in sides:
        count, length = (lax.axis_size(axis), array.shape[dim])
        up = [(i, (i + 1) % count) for i in range(count)]
        down = [(j, i) for i, j in up]
        last = lax.slice_in_dim(array, length - width, length, axis=dim)
        first = lax.slice_in_dim(array, 0, width, axis=dim)
        before = lax.ppermute(last, axis, up)
        after = lax.ppermute(first, axis, down)
        array = jnp.concatenate([before, array, after], axis=dim)
    return array


def peskin_weight(distance):
    magnitude = jnp.abs(distance)
    inner = (
        3.0 - 2.0 * magnitude + jnp.sqrt(1.0 + 4.0 * magnitude - 4.0 * magnitude * magnitude)
    ) / 8.0
    outer = (
        5.0 - 2.0 * magnitude - jnp.sqrt(-7.0 + 12.0 * magnitude - 4.0 * magnitude * magnitude)
    ) / 8.0
    return jnp.where(magnitude < 1.0, inner, outer)


def stencil_matrix(cells, offsets, first_row, rows):
    line = lax.broadcasted_iota(jnp.int32, (rows, cells.shape[0]), 0)
    relative = cells - first_row
    matrix = jnp.zeros((rows, cells.shape[0]), jnp.float32)
    for shift_value in OFFSETS:
        weight_row = peskin_weight(shift_value - offsets)
        matrix = matrix + jnp.where(
            line == relative[None, :] + shift_value, weight_row[None, :], 0.0
        )
    return matrix


def slot_matrices(group, x_first, y_first, x_rows, y_rows, depth):
    flat = jnp.moveaxis(group, 1, 0).reshape(group.shape[1], -1)
    cells = flat[0:3].astype(jnp.int32)
    x_matrix = stencil_matrix(cells[0], flat[3], x_first, x_rows)
    y_matrix = stencil_matrix(cells[1], flat[4], y_first, y_rows).astype(jnp.bfloat16)
    z_matrix = stencil_matrix(cells[2], flat[5], 0, depth)
    return (flat[6:9], x_matrix, y_matrix, z_matrix)


def fold_ghosts(padded, axis, size):
    core = lax.slice_in_dim(padded, 4, size + 4, axis=axis)
    low_part = lax.slice_in_dim(padded, 0, 2, axis=axis)
    high_part = lax.slice_in_dim(padded, size + 6, size + 8, axis=axis)
    head = lax.slice_in_dim(core, 0, 2, axis=axis) + low_part
    middle = lax.slice_in_dim(core, 2, size - 2, axis=axis)
    tail = lax.slice_in_dim(core, size - 2, size, axis=axis) + high_part
    return jnp.concatenate([head, middle, tail], axis=axis)


def relax(padded_field, padded_visc):
    center_field = padded_field[:, :, 1:-1, 1:-1]
    center_visc = padded_visc[:, :, 1:-1, 1:-1]

    def face(neighbor_field, neighbor_visc):
        return 0.5 * (center_visc + neighbor_visc) * (neighbor_field - center_field)

    total = face(padded_field[:, :, :-2, 1:-1], padded_visc[:, :, :-2, 1:-1])
    total = total + face(padded_field[:, :, 2:, 1:-1], padded_visc[:, :, 2:, 1:-1])
    total = total + face(padded_field[:, :, 1:-1, :-2], padded_visc[:, :, 1:-1, :-2])
    total = total + face(padded_field[:, :, 1:-1, 2:], padded_visc[:, :, 1:-1, 2:])
    vertical = center_field[:, 1:] - center_field[:, :-1]
    vertical = 0.5 * (center_visc[:, 1:] + center_visc[:, :-1]) * vertical
    zeros_layer = jnp.zeros_like(vertical[:, :1])
    z_term = jnp.concatenate([vertical, zeros_layer], axis=1) - jnp.concatenate(
        [zeros_layer, vertical], axis=1
    )
    return center_field + (total + z_term)


def body(velocity, viscosity, marker_cells, marker_offset, marker_force):
    depth = velocity.shape[1]
    width_x = velocity.shape[2]
    width_y = velocity.shape[3]
    markers = marker_cells.shape[2]
    column_size = lax.axis_size("gy")
    my_row = lax.axis_index("gy")
    x_first = lax.axis_index("gx") * width_x - 2
    y_first = my_row * width_y - 2
    packed = jnp.concatenate(
        [marker_cells.astype(jnp.float32), marker_offset, marker_force], axis=1
    )
    slots = column_size * CAP
    column = lax.all_gather(packed, "gy", axis=0, tiled=True)
    owner_row = column[:, 1, 0].astype(jnp.int32) // width_y
    is_mine = owner_row == my_row
    chosen = jnp.argsort(jnp.where(is_mine, 0, 1), stable=True)[:slots]
    kept_flag = is_mine[chosen].astype(jnp.float32)
    received = column[chosen] * kept_flag[:, None, None]
    grouped = received.reshape(-1, group_slots, received.shape[1], markers)
    x_rows = width_x + 4
    y_rows = width_y + 4

    def spread_group(total, group):
        forces, x_matrix, y_matrix, z_matrix = slot_matrices(
            group, x_first, y_first, x_rows, y_rows, depth
        )
        lifted = (
            forces[:, None, None, :] * z_matrix[None, :, None, :] * x_matrix[None, None, :, :]
        ).astype(jnp.bfloat16)
        lifted = lifted.reshape(-1, lifted.shape[-1])
        product = lax.dot_general(
            lifted, y_matrix, (((1,), (1,)), ((), ())), preferred_element_type=jnp.float32
        )
        return (total + product, None)

    spread_init = jnp.zeros((3 * depth * x_rows, y_rows), jnp.float32)
    spread_sum, _ = lax.scan(spread_group, spread_init, grouped)
    force_padded = spread_sum.reshape(3, depth, x_rows, y_rows)
    gathered_ghosts = padded_2(force_padded, (("gx", 2), ("gy", 3)), 2)
    force_field = fold_ghosts(fold_ghosts(gathered_ghosts, 2, width_x), 3, width_y)
    lifted_visc = viscosity[None]
    padded_field, padded_visc = (
        padded_2(velocity, (("gx", 2), ("gy", 3)), 1),
        padded_2(lifted_visc, (("gx", 2), ("gy", 3)), 1),
    )
    first_field = relax(padded_field, padded_visc)
    refreshed = padded_2(first_field, (("gx", 2), ("gy", 3)), 1)
    second_field = relax(refreshed, padded_visc)
    final_field = second_field + force_field
    rim_field = padded_2(final_field.astype(jnp.bfloat16), (("gx", 2), ("gy", 3)), 2)
    rounded_flat = rim_field.reshape(-1, y_rows)

    def sample_group(carry, group):
        unused_forces, x_matrix, y_matrix, z_matrix = slot_matrices(
            group, x_first, y_first, x_rows, y_rows, depth
        )
        along_y = jnp.dot(rounded_flat, y_matrix, preferred_element_type=jnp.float32)
        along_y = along_y.reshape(3, depth, x_rows, -1)
        values = jnp.sum(
            along_y * z_matrix[None, :, None, :] * x_matrix[None, None, :, :], axis=(1, 2)
        )
        return (carry, jnp.moveaxis(values.reshape(3, group_slots, markers), 0, 1))

    _, sampled = lax.scan(sample_group, jnp.zeros((), jnp.float32), grouped)
    sampled = sampled.reshape(slots, 3, markers)
    spread_back = (
        jnp.zeros((column.shape[0], 3, markers), jnp.float32)
        .at[chosen]
        .add(sampled * kept_flag[:, None, None])
    )
    marker_velocity = lax.psum_scatter(spread_back, "gy", scatter_dimension=0, tiled=True)
    return (final_field, marker_velocity)


def solution(mesh):
    in_specs = (
        P(None, None, "gx", "gy"),
        P(None, "gx", "gy"),
        P(("gx", "gy"), None, None),
        P(("gx", "gy"), None, None),
        P(("gx", "gy"), None, None),
    )
    out_specs = (P(None, None, "gx", "gy"), P(("gx", "gy"), None, None))
    return jax.shard_map(body, mesh=mesh, in_specs=in_specs, out_specs=out_specs, check_vma=False)
```

profile of v0, /device:TPU:1, one launch (start us, length us, event | category | flops | bytes accessed | tf_op | source)
XLA Modules:
  0.0 853.1 jit_solution(3252362983962150139)
XLA Ops:
  52.5 28.9 %all-gather.2.cloned.1.call-done = f32[1024,9,128]{2,0,1:T(8,128)} async-done(((f32[32,9,128]{2,0,1:T(8,128)}), f32[1024,9,128]{2,0,1:T(8,128)}) %all-gather.2.cloned.1.call-update) | async-done | bytes 4718608 | tf_op jit(solution)/shard_map/all_gather | solution.py:99
  87.0 8.6 %copy.27 = f32[1024,9,128]{2,1,0:T(8,128)} copy(f32[1024,9,128]{2,0,1:T(8,128)} %all-gather.2.cloned.1.call-done) | data formatting | bytes 9437184 | tf_op jit(solution)/shard_map/all_gather | solution.py:99
  101.4 98.2 %while.22 = (s32[]{:T(128)}, f32[1920,132]{0,1:T(8,128)S(1)}, f32[16,4,9,128]{3,1,2,0:T(4,128)}, s32[]{:T(128)}, s32[]{:T(128)}, /*index=5*/s32[]{:T(128)}, s32[]{:T(128)}) while((s32[]{:T(128)}, f32[1920,132]{0,1:T(8,128)S(1)}, f32[16,4,9,128]{3,1,2,0:T(4,128)}, s32[]{:T(128)}, s32[]{:T(128)}, /*index=5*/s32[]{:T(128)}, ...), condition=%wide.region_2.3_spmd.clone, body=%wide.region_1.2_spmd.clone.sunk | while | flops 263266304 | bytes 10688619 | solution.py:123
  256.5 8.9 %collective-permute-start.19 = (bf16[3,32,20,2]{1,3,2,0:T(2,128)(2,1)S(1)}, bf16[3,32,20,2]{1,3,2,0:T(2,128)(2,1)S(1)}, u32[]{:S(2)}, u32[]{:S(2)}) collective-permute-start(bf16[3,32,20,2]{1,3,2,0:T(2,128)(2,1)S(1)} %copy.35), channel_id=1, source_target_pairs={{1,0},{2,1},{3,2},{4,3},{5,4},{6,5},{7,6},{8,7},{9,8},{10,9},{11,1... | collective-permute-start | bytes 23048 | tf_op jit(solution)/shard_map/ppermute | solution.py:19
  272.0 275.1 %while.21 = (s32[]{:T(128)}, f32[16,4,3,128]{3,2,1,0:T(4,128)S(1)}, f32[16,4,9,128]{3,1,2,0:T(4,128)}, s32[]{:T(128)}, bf16[1920,132]{1,0:T(8,128)(2,1)S(1)}, /*index=5*/s32[]{:T(128)}, s32[]{:T(128)}) while((s32[]{:T(128)}, f32[16,4,3,128]{3,2,1,0:T(4,128)S(1)}, f32[16,4,9,128]{3,1,2,0:T(4,128)}, s32[]{:T(128)}, ...), condition=%wide.region_5.6_spmd, body=%wide.region_3.5_spmd.sunk | while | flops 263691776 | bytes 24585316 | solution.py:150
  275.6 5.6 copy.51
  281.2 4.9 reshape.1370
  292.8 5.6 copy.51
  298.4 4.9 reshape.1370
  310.0 5.6 copy.51
  327.2 5.6 copy.51
  344.4 5.6 copy.51
  361.6 5.6 copy.51
  378.8 5.6 copy.51
  396.0 5.6 copy.51
  413.2 5.6 copy.51
  430.4 5.6 copy.51
  447.6 5.6 copy.51
  464.8 5.6 copy.51
  481.9 5.6 copy.51
  499.1 5.6 copy.51
  516.3 5.6 copy.51
  533.5 5.6 copy.51
  553.0 291.5 %all-reduce.7.cloned.1.call-done = f32[1024,3,128]{2,1,0:T(4,128)} async-done(((f32[1024,3,128]{2,1,0:T(4,128)}), f32[1024,3,128]{2,1,0:T(4,128)}) %all-reduce.7.cloned.1.call-update) | async-done | bytes 1572880
  (624 shorter events, 398.2 us)
Async XLA Ops:
  7.2 74.2 %all-gather.2.cloned.1.call-start = ((), (), s32[]{:S(2)}) async-start(), calls=%async_computation | async-start | bytes 4866048 | tf_op jit(solution)/shard_map/all_gather | solution.py:99
  9.6 834.9 %all-reduce.7.cloned.1.call-start = ((), (), s32[]{:S(2)}) async-start(), calls=%async_computation.1 | async-start | bytes 4194304
  10.8 19.0 %collective-permute-start.3 = (f32[3,32,1,128]{3,2,1,0:T(1,128)S(1)}, f32[3,32,1,128]{3,2,1,0:T(1,128)S(1)}, u32[]{:S(2)}, u32[]{:S(2)}) collective-permute-start(f32[3,32,1,128]{3,2,1,0:T(1,128)S(1)} %get-tuple-element.206), channel_id=1, source_target_pairs={{32,0},{64,32},{96,64},{128,96},{160,128},{192,160},{224,192},{0,2... | collective-permute-start | bytes 147464 | tf_op jit(solution)/shard_map/ppermute | solution.py:19
  15.6 14.3 %collective-permute-start.1 = (f32[3,32,1,128]{3,2,1,0:T(1,128)S(1)}, f32[3,32,1,128]{3,2,1,0:T(1,128)S(1)}, u32[]{:S(2)}, u32[]{:S(2)}) collective-permute-start(f32[3,32,1,128]{3,2,1,0:T(1,128)S(1)} %get-tuple-element.205), channel_id=1, source_target_pairs={{0,32},{32,64},{64,96},{96,128},{128,160},{160,192},{192,224},{224... | collective-permute-start | bytes 147464 | tf_op jit(solution)/shard_map/ppermute | solution.py:18
  16.6 4.9 collective-permute-start.2
  20.2 4.7 collective-permute-start
  26.0 12.5 %collective-permute-start.4 = (f32[1,32,18,1]{3,2,1,0:T(8,128)}, f32[1,32,18,1]{3,2,1,0:T(8,128)S(1)}, u32[]{:S(2)}, u32[]{:S(2)}) collective-permute-start(f32[1,32,18,1]{3,2,1,0:T(8,128)} %get-tuple-element.211), channel_id=1, source_target_pairs={{0,1},{1,2},{2,3},{3,4},{4,5},{5,6},{6,7},{7,8},{8,9},{9,10},{10,1... | collective-permute-start | bytes 6920 | tf_op jit(solution)/shard_map/ppermute | solution.py:18
  29.8 8.7 %collective-permute-start.6 = (f32[1,32,18,1]{3,2,1,0:T(8,128)}, f32[1,32,18,1]{3,2,1,0:T(8,128)}, u32[]{:S(2)}, u32[]{:S(2)}) collective-permute-start(f32[1,32,18,1]{3,2,1,0:T(8,128)} %get-tuple-element.212), channel_id=1, source_target_pairs={{1,0},{2,1},{3,2},{4,3},{5,4},{6,5},{7,6},{8,7},{9,8},{10,9},{11,1... | collective-permute-start | bytes 6920 | tf_op jit(solution)/shard_map/ppermute | solution.py:19
  33.1 7.7 collective-permute-start.7
  38.4 2.9 collective-permute-start.5
  45.6 3.3 collective-permute-start.9
  45.8 5.5 collective-permute-start.8
  49.0 46.7 %copy-start.18 = (f32[3,32,1,128]{3,2,1,0:T(1,128)}, f32[3,32,1,128]{3,2,1,0:T(1,128)S(1)}, u32[]{:S(2)}) copy-start(f32[3,32,1,128]{3,2,1,0:T(1,128)S(1)} %collective-permute-done.9) | copy-start | bytes 147460
  51.3 44.3 %copy-start.20 = (f32[3,32,1,128]{3,2,1,0:T(1,128)}, f32[3,32,1,128]{3,2,1,0:T(1,128)S(1)}, u32[]{:S(2)}) copy-start(f32[3,32,1,128]{3,2,1,0:T(1,128)S(1)} %collective-permute-done.8) | copy-start | bytes 147460
  204.1 8.6 %collective-permute-start.13 = (f32[3,32,2,132]{3,2,1,0:T(2,128)}, f32[3,32,2,132]{3,2,1,0:T(2,128)}, u32[]{:S(2)}, u32[]{:S(2)}) collective-permute-start(f32[3,32,2,132]{3,2,1,0:T(2,128)} %get-tuple-element.196), channel_id=1, source_target_pairs={{32,0},{64,32},{96,64},{128,96},{160,128},{192,160},{224,192},{0,2... | collective-permute-start | bytes 304136 | tf_op jit(solution)/shard_map/ppermute | solution.py:19
  205.8 8.4 collective-permute-start.12
  210.0 15.0 %collective-permute-start.11 = (f32[3,32,18,1]{1,3,2,0:T(1,128)}, f32[3,32,18,1]{1,3,2,0:T(1,128)}, u32[]{:S(2)}, u32[]{:S(2)}) collective-permute-start(f32[3,32,18,1]{1,3,2,0:T(1,128)} %copy.25), channel_id=1, source_target_pairs={{1,0},{2,1},{3,2},{4,3},{5,4},{6,5},{7,6},{8,7},{9,8},{10,9},{11,1... | collective-permute-start | bytes 20744 | tf_op jit(solution)/shard_map/ppermute | solution.py:19
  211.7 15.6 %collective-permute-start.10 = (f32[3,32,18,1]{1,3,2,0:T(1,128)}, f32[3,32,18,1]{1,3,2,0:T(1,128)}, u32[]{:S(2)}, u32[]{:S(2)}) collective-permute-start(f32[3,32,18,1]{1,3,2,0:T(1,128)} %copy.23), channel_id=1, source_target_pairs={{0,1},{1,2},{2,3},{3,4},{4,5},{5,6},{6,7},{7,8},{8,9},{9,10},{10,1... | collective-permute-start | bytes 20744 | tf_op jit(solution)/shard_map/ppermute | solution.py:18
  219.3 10.2 %collective-permute-start.15 = (f32[3,32,24,2]{1,2,3,0:T(8,128)S(1)}, f32[3,32,24,2]{1,2,3,0:T(8,128)S(1)}, u32[]{:S(2)}, u32[]{:S(2)}) collective-permute-start(f32[3,32,24,2]{1,2,3,0:T(8,128)S(1)} %copy.31), channel_id=1, source_target_pairs={{1,0},{2,1},{3,2},{4,3},{5,4},{6,5},{7,6},{8,7},{9,8},{10,9},{11,1... | collective-permute-start | bytes 55304 | tf_op jit(solution)/shard_map/ppermute | solution.py:19
  223.3 7.8 collective-permute-start.14
  247.8 3.8 collective-permute-start.17
  250.4 5.0 collective-permute-start.16
  256.5 9.8 %collective-permute-start.19 = (bf16[3,32,20,2]{1,3,2,0:T(2,128)(2,1)S(1)}, bf16[3,32,20,2]{1,3,2,0:T(2,128)(2,1)S(1)}, u32[]{:S(2)}, u32[]{:S(2)}) collective-permute-start(bf16[3,32,20,2]{1,3,2,0:T(2,128)(2,1)S(1)} %copy.35), channel_id=1, source_target_pairs={{1,0},{2,1},{3,2},{4,3},{5,4},{6,5},{7,6},{8,7},{9,8},{10,9},{11,1... | collective-permute-start | bytes 23048 | tf_op jit(solution)/shard_map/ppermute | solution.py:19
  265.9 4.0 collective-permute-start.18
  (23 other events, 101.3 us)
Sparse Core Ops, SparseCore 0:
  10.6 70.7 all-gather.1
  551.8 292.6 all-reduce.6
where the time goes:
time: 868 us; the launch traced here: 853 us
  waiting for transfers between devices  337 us (39%)
  local copies, waits for them, and re-layouts  279 us (32%)
  other arithmetic  99.6 us (11%)
  matrix products  82.7 us (10%)
  starting transfers between devices  36.6 us (4%)
  between operations  15.4 us (2%)
    unnamed x3, waiting for transfers between devices  292 us
    dot_general x16, local copies, waits for them, and re-layouts, sample_group(): jnp.dot(rounded_flat, y_matrix, preferred_element_type=jnp.float32)  88.9 us
    reshape x16, local copies, waits for them, and re-layouts, sample_group(): along_y = along_y.reshape(3, depth, x_rows, -1)  77.9 us
    reduce_sum x16, other arithmetic, sample_group(): jnp.sum(along_y * z_matrix[None, :, None, :] * x_matrix[None, None, :, :]...  48.3 us
    dot_general x16, matrix products, sample_group(): jnp.dot(rounded_flat, y_matrix, preferred_element_type=jnp.float32)  43.1 us
    dot_general x16, matrix products, spread_group(): lax.dot_general(lifted, y_matrix, (((1,), (1,)), ((), ())), preferred_ele...  39.6 us
    convert_element_type x16, local copies, waits for them, and re-layouts, spread_group(): lifted = (forces[:, None, None, :] * z_matrix[None, :, None, :] * x_matri...  31.8 us
    ppermute x10, starting transfers between devices, padded_2(): after = lax.ppermute(first, axis, down)  28.9 us
  transfers between devices with their start and end apart: 22, of which 11 were waited for; matrix products, arithmetic and copies ran while one was open for 4% of the time, Pallas kernels for 0%

commit v1 on v0

--- a/solution.py
+++ b/solution.py
@@ -96,7 +96,9 @@
         [marker_cells.astype(jnp.float32), marker_offset, marker_force], axis=1
     )
     slots = column_size * CAP
-    column = lax.all_gather(packed, "gy", axis=0, tiled=True)
+    column = jnp.concatenate(
+        lax.all_to_all(jnp.stack([packed] * lax.axis_size("gy")), "gy", 0, 0), axis=0
+    )
     owner_row = column[:, 1, 0].astype(jnp.int32) // width_y
     is_mine = owner_row == my_row
     chosen = jnp.argsort(jnp.where(is_mine, 0, 1), stable=True)[:slots]

time: 868 us -> 951 us (1.096)
  waiting for transfers between devices: 337 us -> 404 us
  starting transfers between devices: 36.6 us -> 53.4 us
    ppermute x10, waiting for transfers between devices: 2.89 us -> 96.5 us  [padded_2(): after = lax.ppermute(first, axis, down)]
    all_gather x1 -> x0, waiting for transfers between devices: 28.9 us -> none  [body(): column = lax.all_gather(packed, 'gy', axis=0, tiled=True)]
    all_to_all x0 -> x1, starting transfers between devices: none -> 12.9 us  [body(): lax.all_to_all(jnp.stack([packed] * lax.axis_size('gy')), 'gy', 0, 0)]
    unnamed x3 -> x2, waiting for transfers between devices: 292 us -> 292 us
  transfers between devices with their start and end apart: 22 -> 22, of which waited for: 11 -> 9; matrix products, arithmetic and copies ran while one was open for 4% -> 4% of each run, Pallas kernels for 0% -> 0%
where the time goes in v1:
time: 951 us; the launch traced here: 935 us
  waiting for transfers between devices  404 us (42%)
  local copies, waits for them, and re-layouts  280 us (29%)
  other arithmetic  96.7 us (10%)
  matrix products  82.9 us (9%)
  starting transfers between devices  53.4 us (6%)
  between operations  15.5 us (2%)
    unnamed x2, waiting for transfers between devices  292 us
    ppermute x10, waiting for transfers between devices, padded_2(): after = lax.ppermute(first, axis, down)  96.5 us
    dot_general x16, local copies, waits for them, and re-layouts, sample_group(): jnp.dot(rounded_flat, y_matrix, preferred_element_type=jnp.float32)  89 us
    reshape x16, local copies, waits for them, and re-layouts, sample_group(): along_y = along_y.reshape(3, depth, x_rows, -1)  77.9 us
    reduce_sum x16, other arithmetic, sample_group(): jnp.sum(along_y * z_matrix[None, :, None, :] * x_matrix[None, None, :, :]...  48.3 us
    dot_general x16, matrix products, sample_group(): jnp.dot(rounded_flat, y_matrix, preferred_element_type=jnp.float32)  43.2 us
    dot_general x16, matrix products, spread_group(): lax.dot_general(lifted, y_matrix, (((1,), (1,)), ((), ())), preferred_ele...  39.7 us
    ppermute x10, starting transfers between devices, padded_2(): after = lax.ppermute(first, axis, down)  34.7 us
  transfers between devices with their start and end apart: 22, of which 9 were waited for; matrix products, arithmetic and copies ran while one was open for 4% of the time, Pallas kernels for 0%

profile of v1, /device:TPU:1, one launch (start us, length us, event | category | flops | bytes accessed | tf_op | source)
XLA Modules:
  0.0 935.5 jit_solution(15718769690185865104)
XLA Ops:
  11.6 12.9 %all-to-all-start = ((f32[32,32,9,128]{3,1,2,0:T(8,128)}), f32[32,32,9,128]{3,1,2,0:T(8,128)}, u32[]{:S(2)}, u32[]{:S(2)}) async-start(f32[32,32,9,128]{3,1,2,0:T(8,128)} %stack.2), calls=%async_computation | async-start | bytes 9437184 | tf_op jit(solution)/shard_map/all_to_all | solution.py:100
  31.5 94.2 %collective-permute-done.2 = f32[1,32,1,128]{3,2,1,0:T(1,128)S(1)} collective-permute-done((f32[1,32,1,128]{3,2,1,0:T(1,128)S(1)}, f32[1,32,1,128]{3,2,1,0:T(1,128)S(1)}, u32[]{:S(2)}, u32[]{:S(2)}) %collective-permute-start.2) | collective-permute-done | bytes 16416 | tf_op jit(solution)/shard_map/ppermute | solution.py:19
  159.4 6.3 copy.32
  176.1 98.4 %while.22 = (s32[]{:T(128)}, f32[1920,132]{0,1:T(8,128)S(1)}, f32[16,4,9,128]{3,1,0,2:T(4,128)}, s32[]{:T(128)}, s32[]{:T(128)}, /*index=5*/s32[]{:T(128)}, s32[]{:T(128)}) while((s32[]{:T(128)}, f32[1920,132]{0,1:T(8,128)S(1)}, f32[16,4,9,128]{3,1,0,2:T(4,128)}, s32[]{:T(128)}, s32[]{:T(128)}, /*index=5*/s32[]{:T(128)}, ...), condition=%wide.region_2.3_spmd.clone, body=%wide.region_1.2_spmd.clone.sunk | while | flops 263266304 | bytes 10688619 | solution.py:125
  284.7 7.9 collective-permute-start.11
  338.2 8.7 collective-permute-start.19
  353.5 275.3 %while.21 = (s32[]{:T(128)}, f32[16,4,3,128]{3,2,1,0:T(4,128)S(1)}, f32[16,4,9,128]{3,1,0,2:T(4,128)}, s32[]{:T(128)}, bf16[1920,132]{1,0:T(8,128)(2,1)S(1)}, /*index=5*/s32[]{:T(128)}, s32[]{:T(128)}) while((s32[]{:T(128)}, f32[16,4,3,128]{3,2,1,0:T(4,128)S(1)}, f32[16,4,9,128]{3,1,0,2:T(4,128)}, s32[]{:T(128)}, ...), condition=%wide.region_5.6_spmd, body=%wide.region_3.5_spmd.sunk | while | flops 263691776 | bytes 24585316 | solution.py:152
  357.1 5.6 copy.57
  374.3 5.6 copy.57
  391.5 5.6 copy.57
  408.7 5.6 copy.57
  425.9 5.6 copy.57
  443.2 5.6 copy.57
  460.4 5.6 copy.57
  477.6 5.6 copy.57
  494.8 5.6 copy.57
  512.0 5.6 copy.57
  529.2 5.6 copy.57
  546.4 5.6 copy.57
  563.6 5.6 copy.57
  580.8 5.6 copy.57
  598.0 5.6 copy.57
  615.2 5.6 copy.57
  634.7 292.2 %all-reduce.7.cloned.1.call-done = f32[1024,3,128]{2,1,0:T(4,128)} async-done(((f32[1024,3,128]{2,1,0:T(4,128)}), f32[1024,3,128]{2,1,0:T(4,128)}) %all-reduce.7.cloned.1.call-update) | async-done | bytes 1572880
  (626 shorter events, 405.8 us)
Async XLA Ops:
  11.6 16.1 %copy-start.10 = (f32[32,16,128]{2,1,0:T(8,128)S(1)}, f32[32,16,128]{2,1,0:T(8,128)}, u32[]{:S(2)}) copy-start(f32[32,16,128]{2,1,0:T(8,128)} %param.10) | copy-start | bytes 786436
  11.6 144.9 %all-to-all-start = ((f32[32,32,9,128]{3,1,2,0:T(8,128)}), f32[32,32,9,128]{3,1,2,0:T(8,128)}, u32[]{:S(2)}, u32[]{:S(2)}) async-start(f32[32,32,9,128]{3,1,2,0:T(8,128)} %stack.2), calls=%async_computation | async-start | bytes 9437184 | tf_op jit(solution)/shard_map/all_to_all | solution.py:100
  24.5 902.4 %all-reduce.7.cloned.1.call-start = ((), (), s32[]{:S(2)}) async-start(), calls=%async_computation.1 | async-start | bytes 4194304
  24.7 109.4 %collective-permute-start.3 = (f32[3,32,1,128]{3,2,1,0:T(1,128)S(1)}, f32[3,32,1,128]{3,2,1,0:T(1,128)S(1)}, u32[]{:S(2)}, u32[]{:S(2)}) collective-permute-start(f32[3,32,1,128]{3,2,1,0:T(1,128)S(1)} %get-tuple-element.224), channel_id=1, source_target_pairs={{32,0},{64,32},{96,64},{128,96},{160,128},{192,160},{224,192},{0,2... | collective-permute-start | bytes 147464 | tf_op jit(solution)/shard_map/ppermute | solution.py:19
  27.7 106.4 %collective-permute-start.1 = (f32[3,32,1,128]{3,2,1,0:T(1,128)S(1)}, f32[3,32,1,128]{3,2,1,0:T(1,128)S(1)}, u32[]{:S(2)}, u32[]{:S(2)}) collective-permute-start(f32[3,32,1,128]{3,2,1,0:T(1,128)S(1)} %get-tuple-element.223), channel_id=1, source_target_pairs={{0,32},{32,64},{64,96},{96,128},{128,160},{160,192},{192,224},{224... | collective-permute-start | bytes 147464 | tf_op jit(solution)/shard_map/ppermute | solution.py:18
  27.7 98.0 %collective-permute-start.2 = (f32[1,32,1,128]{3,2,1,0:T(1,128)S(1)}, f32[1,32,1,128]{3,2,1,0:T(1,128)S(1)}, u32[]{:S(2)}, u32[]{:S(2)}) collective-permute-start(f32[1,32,1,128]{3,2,1,0:T(1,128)S(1)} %get-tuple-element.236), channel_id=1, source_target_pairs={{32,0},{64,32},{96,64},{128,96},{160,128},{192,160},{224,192},{0,2... | collective-permute-start | bytes 49160 | tf_op jit(solution)/shard_map/ppermute | solution.py:19
  31.4 99.8 %collective-permute-start = (f32[1,32,1,128]{3,2,1,0:T(1,128)S(1)}, f32[1,32,1,128]{3,2,1,0:T(1,128)S(1)}, u32[]{:S(2)}, u32[]{:S(2)}) collective-permute-start(f32[1,32,1,128]{3,2,1,0:T(1,128)S(1)} %get-tuple-element.235), channel_id=1, source_target_pairs={{0,32},{32,64},{64,96},{96,128},{128,160},{160,192},{192,224},{224... | collective-permute-start | bytes 49160 | tf_op jit(solution)/shard_map/ppermute | solution.py:18
  31.4 94.3 %copy-start.16 = (f32[31,16,128]{2,1,0:T(8,128)}, f32[31,16,128]{2,1,0:T(8,128)S(1)}, u32[]{:S(2)}) copy-start(f32[31,16,128]{2,1,0:T(8,128)S(1)} %fusion.244) | copy-start | bytes 761860
  132.2 10.3 %collective-permute-start.4 = (f32[1,32,18,1]{3,2,1,0:T(8,128)}, f32[1,32,18,1]{3,2,1,0:T(8,128)S(1)}, u32[]{:S(2)}, u32[]{:S(2)}) collective-permute-start(f32[1,32,18,1]{3,2,1,0:T(8,128)} %get-tuple-element.229), channel_id=1, source_target_pairs={{0,1},{1,2},{2,3},{3,4},{4,5},{5,6},{6,7},{7,8},{8,9},{9,10},{10,1... | collective-permute-start | bytes 6920 | tf_op jit(solution)/shard_map/ppermute | solution.py:18
  134.1 8.5 collective-permute-start.6
  137.3 7.5 collective-permute-start.7
  142.4 2.9 collective-permute-start.5
  149.6 3.0 collective-permute-start.9
  149.7 5.6 collective-permute-start.8
  279.1 14.7 %collective-permute-start.13 = (f32[3,32,2,132]{3,2,1,0:T(2,128)}, f32[3,32,2,132]{3,2,1,0:T(2,128)}, u32[]{:S(2)}, u32[]{:S(2)}) collective-permute-start(f32[3,32,2,132]{3,2,1,0:T(2,128)} %get-tuple-element.214), channel_id=1, source_target_pairs={{32,0},{64,32},{96,64},{128,96},{160,128},{192,160},{224,192},{0,2... | collective-permute-start | bytes 304136 | tf_op jit(solution)/shard_map/ppermute | solution.py:19
  279.1 14.7 %collective-permute-start.12 = (f32[3,32,2,132]{3,2,1,0:T(2,128)}, f32[3,32,2,132]{3,2,1,0:T(2,128)}, u32[]{:S(2)}, u32[]{:S(2)}) collective-permute-start(f32[3,32,2,132]{3,2,1,0:T(2,128)} %get-tuple-element.213), channel_id=1, source_target_pairs={{0,32},{32,64},{64,96},{96,128},{128,160},{160,192},{192,224},{224... | collective-permute-start | bytes 304136 | tf_op jit(solution)/shard_map/ppermute | solution.py:18
  284.7 22.1 %collective-permute-start.11 = (f32[3,32,18,1]{1,3,2,0:T(1,128)}, f32[3,32,18,1]{1,3,2,0:T(1,128)}, u32[]{:S(2)}, u32[]{:S(2)}) collective-permute-start(f32[3,32,18,1]{1,3,2,0:T(1,128)} %copy.29), channel_id=1, source_target_pairs={{1,0},{2,1},{3,2},{4,3},{5,4},{6,5},{7,6},{8,7},{9,8},{10,9},{11,1... | collective-permute-start | bytes 20744 | tf_op jit(solution)/shard_map/ppermute | solution.py:19
  293.6 15.4 %collective-permute-start.10 = (f32[3,32,18,1]{1,3,2,0:T(1,128)}, f32[3,32,18,1]{1,3,2,0:T(1,128)}, u32[]{:S(2)}, u32[]{:S(2)}) collective-permute-start(f32[3,32,18,1]{1,3,2,0:T(1,128)} %copy.27), channel_id=1, source_target_pairs={{0,1},{1,2},{2,3},{3,4},{4,5},{5,6},{6,7},{7,8},{8,9},{9,10},{10,1... | collective-permute-start | bytes 20744 | tf_op jit(solution)/shard_map/ppermute | solution.py:18
  298.9 12.4 %collective-permute-start.15 = (f32[3,32,24,2]{1,2,3,0:T(8,128)S(1)}, f32[3,32,24,2]{1,2,3,0:T(8,128)S(1)}, u32[]{:S(2)}, u32[]{:S(2)}) collective-permute-start(f32[3,32,24,2]{1,2,3,0:T(8,128)S(1)} %copy.37), channel_id=1, source_target_pairs={{1,0},{2,1},{3,2},{4,3},{5,4},{6,5},{7,6},{8,7},{9,8},{10,9},{11,1... | collective-permute-start | bytes 55304 | tf_op jit(solution)/shard_map/ppermute | solution.py:19
  305.8 7.1 collective-permute-start.14
  329.7 3.4 collective-permute-start.17
  331.9 5.2 collective-permute-start.16
  338.2 9.5 %collective-permute-start.19 = (bf16[3,32,20,2]{1,3,2,0:T(2,128)(2,1)S(1)}, bf16[3,32,20,2]{1,3,2,0:T(2,128)(2,1)S(1)}, u32[]{:S(2)}, u32[]{:S(2)}) collective-permute-start(bf16[3,32,20,2]{1,3,2,0:T(2,128)(2,1)S(1)} %copy.41), channel_id=1, source_target_pairs={{1,0},{2,1},{3,2},{4,3},{5,4},{6,5},{7,6},{8,7},{9,8},{10,9},{11,1... | collective-permute-start | bytes 23048 | tf_op jit(solution)/shard_map/ppermute | solution.py:19
  347.3 4.1 collective-permute-start.18
  (23 other events, 91.7 us)
Sparse Core Ops, SparseCore 0:
  633.5 293.3 all-reduce.6
